TPU v7x, 32 devices: a whole 2x2x4 slice. The times are simulated.
32 devices in a mesh: src: 8 (over y, x, core), dst: 4 (over z).
Axes of the slice: x: 2, y: 2, z: 4, core: 2. Of those that a mesh axis runs over, the one named last changes fastest.
Arguments:
- raw: bfloat16 [4096, 256], P(('src', 'dst')), may hold values from -6 to 6
- enc_w1: bfloat16 [256, 512], replicated, may hold values from -0.375 to 0.375
- enc_w2: bfloat16 [512, 256], replicated, may hold values from -0.25 to 0.25
- block_weights: float32 [512, 128, 128], P(('src', 'dst')), may hold values from -0.125 to 0.125
- block_cols: int32 [512], P(('src', 'dst')), may hold values from 0 to 3, as said below
- noise: bfloat16 [3, 4096, 256], P(None, ('src', 'dst')), may hold values from -3 to 3
Outputs:
- encoded: bfloat16 [4096, 256], P(('src', 'dst'))
- hops: bfloat16 [3, 4096, 256], P(None, ('src', 'dst'))
Inputs may be any that keep to these rules, and one draw needn't show every extreme that they name: `block_cols`: entry b of each device's 16 entries belongs to row block b // 2; row blocks 2j and 2j+1 of a device together name every column block exactly once, each naming 4 // 2 distinct ones.
All inputs are finite; a program needn't handle non-finite values.
Results may differ from a plain program's by a relative error of at most 0.0058.
Values may be sent and summed in bfloat16 or wider, within the bound.
A program may use at most 128 MiB of HBM per device.

v0:
```python
import functools

import jax
import jax.numpy as jnp
from jax import lax
from jax.experimental import pallas as pl
from jax.experimental.pallas import tpu as pltpu
from jax.sharding import PartitionSpec as P

MESH = pl.DeviceIdType.MESH
CHUNKS = 2
F32 = jnp.float32
BF16 = jnp.bfloat16


def shifted(me, step, count):
    if count & (count - 1) == 0:
        return me ^ step, me ^ step
    return lax.rem(me + step, count), lax.rem(me + count - step, count)


def kernel(
    n_src, n_dst, hops,
    raw_h, w1_h, w2_h, bw_h, cols, noise_h,
    enc_h, hops_h,
    raw_v, w1_v, w2_v, bw_v, noise_v, enc_v, hops_v, wcat, gath, out1, in1, out2, in2, acc,
    load_sem, store_sem, g_send, g_recv, send1, recv1, send2, recv2,
):
    src, dst = lax.axis_index("src"), lax.axis_index("dst")
    pairs = n_src // 2
    pair, core = src // 2, lax.rem(src, 2)
    partner = pair * 2 + 1 - core
    side = bw_v.shape[1]
    per_row = bw_v.shape[0] // n_src
    width = enc_v.shape[1]
    part = width // CHUNKS

    barrier = pltpu.get_barrier_semaphore()
    greeted = 0
    for step in range(1, n_dst):
        to, _ = shifted(dst, step, n_dst)
        pl.semaphore_signal(barrier, inc=1, device_id={"dst": to}, device_id_type=MESH)
        greeted += 1
    for step in range(1, pairs):
        to, _ = shifted(pair, step, pairs)
        pl.semaphore_signal(barrier, inc=1, device_id={"src": to * 2 + core}, device_id_type=MESH)
        greeted += 1
    pl.semaphore_signal(barrier, inc=1, device_id={"src": partner}, device_id_type=MESH)
    greeted += 1

    loads = [
        pltpu.make_async_copy(a, b, load_sem.at[i])
        for i, (a, b) in enumerate(
            ((raw_h, raw_v), (w1_h, w1_v), (w2_h, w2_v), (bw_h, bw_v), (noise_h, noise_v))
        )
    ]
    for load in loads:
        load.start()

    def normalized(z):
        scale = lax.rsqrt(jnp.sum(z * z, axis=-1, keepdims=True) * (1.0 / width) + 1e-06)
        return (z * scale).astype(BF16)

    loads[0].wait()
    loads[1].wait()
    v = jnp.dot(raw_v[...], w1_v[...], preferred_element_type=F32)
    hidden = (v * jax.nn.sigmoid(v)).astype(BF16)
    loads[2].wait()
    feats = normalized(jnp.dot(hidden, w2_v[...], preferred_element_type=F32))
    enc_v[...] = feats
    stores = [pltpu.make_async_copy(enc_v, enc_h, store_sem.at[0])]
    stores[0].start()

    pl.semaphore_wait(barrier, greeted)
    sent = []

    def gather(hop, feats):
        waits = []
        for c in range(CHUNKS):
            gath[hop][c][dst] = feats[:, c * part : (c + 1) * part]
        for c in range(CHUNKS):
            buf = gath[hop][c]
            mine = []
            for step in range(1, n_dst):
                to, _ = shifted(dst, step, n_dst)
                copy = pltpu.make_async_remote_copy(
                    src_ref=buf.at[dst],
                    dst_ref=buf.at[dst],
                    send_sem=g_send.at[hop, c, step - 1],
                    recv_sem=g_recv.at[hop, c, step - 1],
                    device_id={"dst": to},
                    device_id_type=MESH,
                )
                copy.start()
                mine.append(copy)
            waits.append(mine)
            sent.extend(mine)
        return waits

    waits = gather(0, feats)

    loads[3].wait()
    for b in range(bw_v.shape[0]):
        r, i = divmod(b, per_row)
        w = bw_v[b]
        high = w.astype(BF16)
        wcat[r, 0:side, i * side : (i + 1) * side] = high
        wcat[r, side : 2 * side, i * side : (i + 1) * side] = (w - high.astype(F32)).astype(BF16)
    loads[4].wait()

    order = list(reversed(range(pairs)))
    def at(step):
        return shifted(pair, step, pairs)[0] if step else pair

    named = {
        (step, side_core): [
            cols[(at(step) * 2 + (core if side_core else 1 - core)) * per_row + i]
            for i in range(per_row)
        ]
        for step in order
        for side_core in (0, 1)
    }
    for hop in range(hops):
        arrivals = []
        for c in range(CHUNKS):
            buf = gath[hop][c]
            for copy in waits[c]:
                copy.wait_recv()

            def product(row, step, own):
                picked = [buf[name] for name in named[step, own]]
                both = jnp.dot(
                    wcat[row], jnp.concatenate(picked, axis=0), preferred_element_type=F32
                )
                return both[:side] + both[side:]

            first = {}
            for step in order:
                to, _ = shifted(pair, step, pairs) if step else (pair, pair)
                out1[hop, c, step] = product(to * 2 + 1 - core, step, 0).astype(BF16)
                copy = pltpu.make_async_remote_copy(
                    src_ref=out1.at[hop, c, step],
                    dst_ref=in1.at[hop, c, step],
                    send_sem=send1.at[hop, c, step],
                    recv_sem=recv1.at[hop, c, step],
                    device_id={"src": partner},
                    device_id_type=MESH,
                )
                copy.start()
                first[step] = copy
                sent.append(copy)
            second = []
            for step in order:
                to, _ = shifted(pair, step, pairs) if step else (pair, pair)
                mine = product(to * 2 + core, step, 1)
                first[step].wait_recv()
                mine = mine + in1[hop, c, step].astype(F32)
                if step == 0:
                    acc[c] = mine
                    continue
                out2[hop, c, step - 1] = mine.astype(BF16)
                copy = pltpu.make_async_remote_copy(
                    src_ref=out2.at[hop, c, step - 1],
                    dst_ref=in2.at[hop, c, step - 1],
                    send_sem=send2.at[hop, c, step - 1],
                    recv_sem=recv2.at[hop, c, step - 1],
                    device_id={"src": to * 2 + core},
                    device_id_type=MESH,
                )
                copy.start()
                second.append(copy)
                sent.append(copy)
            arrivals.append(second)
        sums = []
        for c in range(CHUNKS):
            z = acc[c] + noise_v[hop, :, c * part : (c + 1) * part].astype(F32)
            for step in range(1, pairs):
                arrivals[c][pairs - 1 - step].wait_recv()
                z = z + in2[hop, c, step - 1].astype(F32)
            sums.append(z)
        feats = normalized(jnp.concatenate(sums, axis=1) if CHUNKS > 1 else sums[0])
        if hop < hops - 1:
            waits = gather(hop + 1, feats)
        hops_v[hop] = feats
        store = pltpu.make_async_copy(hops_v.at[hop], hops_h.at[hop], store_sem.at[hop + 1])
        store.start()
        stores.append(store)
    for copy in sent:
        copy.wait_send()
    for store in stores:
        store.wait()


def finish(enc_i, hops_i, enc_o, hops_o, enc_v, hops_v, sem):
    reads = [
        pltpu.make_async_copy(hops_i, hops_v, sem.at[0]),
        pltpu.make_async_copy(enc_i, enc_v, sem.at[1]),
    ]
    writes = [
        pltpu.make_async_copy(hops_v, hops_o, sem.at[2]),
        pltpu.make_async_copy(enc_v, enc_o, sem.at[3]),
    ]
    for read in reads:
        read.start()
    for read, write in zip(reads, writes):
        read.wait()
        write.start()
    for write in writes:
        write.wait()


def shards(n_src, n_dst, raw, enc_w1, enc_w2, block_weights, block_cols, noise):
    blocks, side, _ = block_weights.shape
    hops, rows, width = noise.shape
    pairs = n_src // 2
    per_row = blocks // n_src
    part = width // CHUNKS
    assert rows == side and n_src % 2 == 0
    anywhere = pl.BlockSpec(memory_space=pl.ANY)
    dma = pltpu.SemaphoreType.DMA
    far = max(pairs - 1, 1)
    near = max(n_dst - 1, 1)
    encoded, kept = pl.pallas_call(
        functools.partial(kernel, n_src, n_dst, hops),
        out_shape=(
            jax.ShapeDtypeStruct((rows, width), BF16),
            jax.ShapeDtypeStruct((hops, rows, width), BF16),
        ),
        in_specs=[anywhere] * 4 + [pl.BlockSpec(memory_space=pltpu.SMEM), anywhere],
        out_specs=(anywhere, anywhere),
        scratch_shapes=[
            pltpu.VMEM(raw.shape, BF16),
            pltpu.VMEM(enc_w1.shape, BF16),
            pltpu.VMEM(enc_w2.shape, BF16),
            pltpu.VMEM(block_weights.shape, F32),
            pltpu.VMEM(noise.shape, BF16),
            pltpu.VMEM((rows, width), BF16),
            pltpu.VMEM((hops, rows, width), BF16),
            pltpu.VMEM((n_src, 2 * side, per_row * side), BF16),
            [[pltpu.VMEM((n_dst, rows, part), BF16) for _ in range(CHUNKS)] for _ in range(hops)],
            pltpu.VMEM((hops, CHUNKS, pairs, rows, part), BF16),
            pltpu.VMEM((hops, CHUNKS, pairs, rows, part), BF16),
            pltpu.VMEM((hops, CHUNKS, far, rows, part), BF16),
            pltpu.VMEM((hops, CHUNKS, far, rows, part), BF16),
            pltpu.VMEM((CHUNKS, rows, part), F32),
            dma((5,)),
            dma((hops + 1,)),
            dma((hops, CHUNKS, near)),
            dma((hops, CHUNKS, near)),
            dma((hops, CHUNKS, pairs)),
            dma((hops, CHUNKS, pairs)),
            dma((hops, CHUNKS, far)),
            dma((hops, CHUNKS, far)),
        ],
        compiler_params=pltpu.CompilerParams(
            collective_id=0, has_side_effects=True, vmem_limit_bytes=60 * 1024 * 1024
        ),
    )(raw, enc_w1, enc_w2, block_weights, block_cols, noise)
    shapes = (
        jax.ShapeDtypeStruct((rows, width), BF16),
        jax.ShapeDtypeStruct((hops, rows, width), BF16),
    )
    return pl.pallas_call(
        finish,
        out_shape=shapes,
        in_specs=[anywhere, anywhere],
        out_specs=(anywhere, anywhere),
        scratch_shapes=[pltpu.VMEM(s.shape, BF16) for s in shapes] + [dma((4,))],
    )(encoded, kept)


def solution(mesh):
    placed = (
        P(("src", "dst"), None),
        P(),
        P(),
        P(("src", "dst"), None, None),
        P(("src", "dst")),
        P(None, ("src", "dst"), None),
    )
    return jax.shard_map(
        functools.partial(shards, mesh.shape["src"], mesh.shape["dst"]),
        mesh=mesh,
        in_specs=placed,
        out_specs=(P(("src", "dst"), None), P(None, ("src", "dst"), None)),
        check_vma=False,
    )
```

profile of v0, /device:TPU:0, one launch (start us, length us, event | category | flops | bytes accessed | tf_op | source)
XLA Modules:
  0.0 46.9 jit_solution(9458505884699949569)
XLA Ops:
  0.6 44.6 %shard_map.77 = (bf16[128,256]{1,0:T(8,128)(2,1)}, bf16[3,128,256]{2,1,0:T(8,128)(2,1)}) custom-call(bf16[128,256]{1,0:T(8,128)(2,1)} %raw_h.1, bf16[256,512]{1,0:T(8,128)(2,1)} %w1_h.1, bf16[512,256]{1,0:T(8,128)(2,1)} %w2_h.1, f32[16,128,128]{2,1,0:T(8,128)} %bw_h.1, s32[16]{0:T(128)} %cols.1, bf16[3,128,256]{2,1,0:T(8,128)(2,1)} %noise_h.1), custom_call_target="tpu_custom_call" | custom-call | tf_op jit(solution)/shard_map/pallas_call | solution.py:223
  45.3 1.7 %shard_map.78 = (bf16[128,256]{1,0:T(8,128)(2,1)}, bf16[3,128,256]{2,1,0:T(8,128)(2,1)}) custom-call(bf16[128,256]{1,0:T(8,128)(2,1)} %get-tuple-element.4.enc_i, bf16[3,128,256]{2,1,0:T(8,128)(2,1)} %get-tuple-element.5.hops_i), custom_call_target="tpu_custom_call" | custom-call | tf_op jit(solution)/shard_map/pallas_call | solution.py:263
where the time goes:
time: 47.1 us; the launch traced here: 46.9 us
  Pallas kernels  46.3 us (98%)
  between operations  0.64 us (1%)
    pallas_call x1, Pallas kernels, shards(): pl.pallas_call(functools.partial(kernel, n_src, n_dst, hops), out_shape=(...  44.6 us
    pallas_call x1, Pallas kernels, shards(): pl.pallas_call(finish, out_shape=shapes, in_specs=[anywhere, anywhere], o...  1.66 us

commit v1 on v0

v1 whole, which is shorter than its diff:
```python
import functools

import jax
import jax.numpy as jnp
from jax import lax
from jax.experimental import pallas as pl
from jax.experimental.pallas import tpu as pltpu
from jax.sharding import PartitionSpec as P

MESH = pl.DeviceIdType.MESH
F32 = jnp.float32
BF16 = jnp.bfloat16


def shifted(me, step, count):
    if count & (count - 1) == 0:
        return me ^ step, me ^ step
    return lax.rem(me + step, count), lax.rem(me + count - step, count)


def kernel(
    n_src, n_dst, hops,
    raw_h, w1_h, w2_h, bw_h, cols, noise_h,
    enc_h, hops_h,
    raw_v, w1_v, w2_v, bw_v, noise_v, enc_v, last_v,
    dense, scaled, gath, cross, acc, out, inn, near_out, near_in,
    noise_p, zs, stat_out, stat_in, scale, kept, kept_in,
    load_sem, store_sem, w_send, w_recv, g_send, g_recv, r_send, r_recv, s_send, s_recv, p_send, p_recv,
):
    src, dst = lax.axis_index("src"), lax.axis_index("dst")
    pairs = n_src // 2
    pair, core = src // 2, lax.rem(src, 2)
    partner = pair * 2 + 1 - core
    side = bw_v.shape[1]
    per_row = bw_v.shape[0] // n_src
    rows, width = enc_v.shape
    half = width // 2
    last = hops - 1

    def at_core(chip, rel):
        return chip * 2 + (1 - core if rel else core)

    def lanes(h):
        return pl.ds(pl.multiple_of(h * half, half), half)

    def remote(a, b, send, recv, to):
        return pltpu.make_async_remote_copy(
            src_ref=a, dst_ref=b, send_sem=send, recv_sem=recv, device_id=to, device_id_type=MESH
        )

    loads = [
        pltpu.make_async_copy(a, b, load_sem.at[i])
        for i, (a, b) in enumerate(
            ((raw_h, raw_v), (w1_h, w1_v), (w2_h, w2_v), (bw_h, bw_v), (noise_h, noise_v))
        )
    ]
    for load in loads:
        load.start()

    to_dst = [shifted(dst, step, n_dst)[0] if step else dst for step in range(n_dst)]
    from_dst = [shifted(dst, step, n_dst)[1] if step else dst for step in range(n_dst)]
    to_pair = [shifted(pair, step, pairs)[0] if step else pair for step in range(pairs)]

    barrier = pltpu.get_barrier_semaphore()
    greeted = 0
    greet = [{"src": partner}]
    for rel in (0, 1):
        greet += [{"src": at_core(pair, rel), "dst": to} for to in to_dst[1:]]
        greet += [{"src": at_core(to, rel)} for to in to_pair[1:]]
    for to in greet:
        pl.semaphore_signal(barrier, inc=1, device_id=to, device_id_type=MESH)
        greeted += 1

    def normalized(z):
        root = lax.rsqrt(jnp.sum(z * z, axis=-1, keepdims=True) * (1.0 / width) + 1e-06)
        return (z * root).astype(BF16)

    sent = []

    def start(copy):
        copy.start()
        sent.append(copy)
        return copy

    far_first = list(reversed(range(1, n_dst)))

    loads[0].wait()
    loads[1].wait()
    v = jnp.dot(raw_v[...], w1_v[...], preferred_element_type=F32)
    hidden = (v * jax.nn.sigmoid(v)).astype(BF16)
    loads[2].wait()
    feats = normalized(jnp.dot(hidden, w2_v[...], preferred_element_type=F32))
    mine = jnp.where(core == 0, feats[:, :half], feats[:, half:])
    gath[0, dst, core] = mine
    cross[...] = jnp.where(core == 0, feats[:, half:], feats[:, :half])
    pl.semaphore_wait(barrier, greeted)
    first = {}
    for step, rel in [(step, rel) for step in far_first for rel in (0, 1)] + [(0, 1)]:
        first[step, rel] = start(
            remote(
                cross if rel else gath.at[0, dst, core],
                gath.at[0, dst, core],
                g_send.at[0, step, rel],
                g_recv.at[0, step, rel],
                {"src": at_core(pair, rel), "dst": to_dst[step]},
            )
        )
    enc_v[...] = feats
    stores = [pltpu.make_async_copy(enc_v, enc_h, store_sem.at[0])]
    stores[0].start()

    loads[3].wait()
    weights = []
    blocks = [[bw_v[r * per_row + i].astype(BF16) for i in range(per_row)] for r in range(n_src)]
    for step in range(n_dst):
        c = from_dst[step]
        for r in range(n_src):
            total = None
            for i in range(per_row):
                term = jnp.where(cols[r * per_row + i] == c, blocks[r][i], jnp.zeros_like(blocks[r][i]))
                total = term if total is None else total + term
            dense[c, core, r] = total
        weights.append(
            start(
                remote(
                    dense.at[c, core], dense.at[c, core], w_send.at[step], w_recv.at[step], {"src": partner}
                )
            )
        )
    loads[4].wait()
    if hops > 1:
        noise_copy = start(
            remote(
                noise_v.at[pl.ds(0, last), :, lanes(1 - core)],
                noise_p,
                p_send.at[3 * hops],
                p_recv.at[3 * hops],
                {"src": partner},
            )
        )

    ones = jnp.ones((8, half), BF16)

    def row_sums(z):
        squares = z * z
        high = squares.astype(BF16)
        low = (squares - high.astype(F32)).astype(BF16)
        dims = (((1,), (1,)), ((), ()))
        return lax.dot_general(ones, high, dims, preferred_element_type=F32) + lax.dot_general(
            ones, low, dims, preferred_element_type=F32
        )

    data = {}
    scales = {}
    pending = None
    scatter_steps = list(reversed(range(1, pairs))) + [0]
    for hop in range(hops):
        for step in range(n_dst):
            c = from_dst[step]
            if hop == 0:
                weights[step].wait_recv()
            else:
                if step:
                    scales[hop, step].wait_recv()
                by = jnp.concatenate([scale[hop - 1, c, 0, 0:1], scale[hop - 1, c, 1, 0:1]], axis=1)
                for r in range(n_src):
                    w = jnp.concatenate([dense[c, 0, r], dense[c, 1, r]], axis=1)
                    scaled[r] = (w.astype(F32) * by).astype(BF16)
            for u in (0, 1):
                if hop == 0:
                    if step or u:
                        first[step, u].wait_recv()
                elif step:
                    data[hop, step, u].wait_recv()
            f = jnp.concatenate([gath[hop, c, 0], gath[hop, c, 1]], axis=0)

            def product(r):
                w = scaled[r] if hop else jnp.concatenate([dense[c, 0, r], dense[c, 1, r]], axis=1)
                return jnp.dot(w, f, preferred_element_type=F32)

            if step < n_dst - 1:
                for r in range(n_src):
                    y = product(r)
                    acc[r] = y if step == 0 else acc[r] + y
            if step == 0 and pending is not None:
                pending()
                pending = None
        copies = {}
        for u in (0, 1):
            for step in scatter_steps:
                to = to_pair[step]
                if hop < last:
                    r = to * 2 + u
                    y = product(r) + acc[r]
                    if step == 0:
                        near_in[u] = y
                        continue
                    out[hop, step - 1, u] = y.astype(BF16)
                    copies[step, u] = start(
                        remote(
                            out.at[hop, step - 1, u],
                            inn.at[hop, step - 1, u],
                            r_send.at[hop, step - 1, u],
                            r_recv.at[hop, step - 1, u],
                            {"src": at_core(to, 0)},
                        )
                    )
                    continue
                rel = 1 - u
                r = at_core(to, rel)
                y = product(r) + acc[r]
                if step == 0 and rel == 0:
                    zs[core] = y
                elif step == 0:
                    near_out[...] = y
                    copies[0, 1] = start(
                        remote(
                            near_out, zs.at[core], p_send.at[3 * hops + 1], p_recv.at[3 * hops + 1], {"src": partner}
                        )
                    )
                else:
                    out[hop, step - 1, rel] = y.astype(BF16)
                    copies[step, rel] = start(
                        remote(
                            out.at[hop, step - 1, rel],
                            inn.at[hop, step - 1, core],
                            r_send.at[hop, step - 1, rel],
                            r_recv.at[hop, step - 1, rel],
                            {"src": r},
                        )
                    )
        if hop == last:
            for copy in copies.values():
                copy.wait_recv()
            sums = []
            for h in range(2):
                z = zs[h] + noise_v[hop, :, h * half : (h + 1) * half].astype(F32)
                for step in range(1, pairs):
                    z = z + inn[hop, step - 1, h].astype(F32)
                sums.append(z)
            last_v[...] = normalized(jnp.concatenate(sums, axis=1))
            stores.append(pltpu.make_async_copy(last_v, hops_h.at[hop], store_sem.at[1]))
            stores[-1].start()
            continue
        if hop == 0:
            noise_copy.wait_recv()
        z_values = []
        for u in (0, 1):
            own_noise = noise_v[hop, :, lanes(core)]
            z = near_in[u] + jnp.where(core == u, own_noise, noise_p[hop]).astype(F32)
            for step in range(1, pairs):
                copies[step, u].wait_recv()
                z = z + inn[hop, step - 1, u].astype(F32)
            gath[hop + 1, dst, u] = z.astype(BF16)
            for step in far_first:
                data[hop + 1, step, u] = start(
                    remote(
                        gath.at[hop + 1, dst, u],
                        gath.at[hop + 1, dst, u],
                        g_send.at[hop + 1, step, u],
                        g_recv.at[hop + 1, step, u],
                        {"dst": to_dst[step]},
                    )
                )
            zs[u] = z
            stat_out[hop, u] = row_sums(z)
        stats = start(
            remote(stat_out.at[hop], stat_in.at[hop], p_send.at[hop], p_recv.at[hop], {"src": partner})
        )
        stats.wait_recv()
        scale[hop, dst] = lax.rsqrt((stat_out[hop] + stat_in[hop]) * (1.0 / width) + 1e-06)
        for step in far_first:
            scales[hop + 1, step] = start(
                remote(
                    scale.at[hop, dst],
                    scale.at[hop, dst],
                    s_send.at[hop, step],
                    s_recv.at[hop, step],
                    {"dst": to_dst[step]},
                )
            )

        def pending(hop=hop):
            for u in (0, 1):
                column = jnp.transpose(jnp.broadcast_to(scale[hop, dst, u, 0:1], (rows, rows)))
                kept[hop, u] = (zs[u] * column).astype(BF16)
            copy = start(
                remote(
                    kept.at[hop, 1 - core],
                    kept_in.at[hop],
                    p_send.at[hops + hop],
                    p_recv.at[hops + hop],
                    {"src": partner},
                )
            )
            store = pltpu.make_async_copy(
                kept.at[hop, core], hops_h.at[hop, :, lanes(core)], store_sem.at[2 + 2 * hop]
            )
            store.start()
            stores.append(store)
            copy.wait_recv()
            store = pltpu.make_async_copy(
                kept_in.at[hop], hops_h.at[hop, :, lanes(1 - core)], store_sem.at[3 + 2 * hop]
            )
            store.start()
            stores.append(store)

    for copy in sent:
        copy.wait_send()
    for store in stores:
        store.wait()


def finish(enc_i, hops_i, enc_o, hops_o, enc_v, hops_v, sem):
    reads = [
        pltpu.make_async_copy(hops_i, hops_v, sem.at[0]),
        pltpu.make_async_copy(enc_i, enc_v, sem.at[1]),
    ]
    writes = [
        pltpu.make_async_copy(hops_v, hops_o, sem.at[2]),
        pltpu.make_async_copy(enc_v, enc_o, sem.at[3]),
    ]
    for read in reads:
        read.start()
    for read, write in zip(reads, writes):
        read.wait()
        write.start()
    for write in writes:
        write.wait()


def shards(n_src, n_dst, raw, enc_w1, enc_w2, block_weights, block_cols, noise):
    blocks, side, _ = block_weights.shape
    hops, rows, width = noise.shape
    pairs = n_src // 2
    half = width // 2
    assert rows == side and n_src % 2 == 0
    anywhere = pl.BlockSpec(memory_space=pl.ANY)
    dma = pltpu.SemaphoreType.DMA
    far = max(pairs - 1, 1)
    mid = max(hops - 1, 1)
    encoded, kept = pl.pallas_call(
        functools.partial(kernel, n_src, n_dst, hops),
        out_shape=(
            jax.ShapeDtypeStruct((rows, width), BF16),
            jax.ShapeDtypeStruct((hops, rows, width), BF16),
        ),
        in_specs=[anywhere] * 4 + [pl.BlockSpec(memory_space=pltpu.SMEM), anywhere],
        out_specs=(anywhere, anywhere),
        scratch_shapes=[
            pltpu.VMEM(raw.shape, BF16),
            pltpu.VMEM(enc_w1.shape, BF16),
            pltpu.VMEM(enc_w2.shape, BF16),
            pltpu.VMEM(block_weights.shape, F32),
            pltpu.VMEM(noise.shape, BF16),
            pltpu.VMEM((rows, width), BF16),
            pltpu.VMEM((rows, width), BF16),
            pltpu.VMEM((n_dst, 2, n_src, side, side), BF16),
            pltpu.VMEM((n_src, side, 2 * side), BF16),
            pltpu.VMEM((hops, n_dst, 2, rows, half), BF16),
            pltpu.VMEM((rows, half), BF16),
            pltpu.VMEM((n_src, rows, half), F32),
            pltpu.VMEM((hops, far, 2, rows, half), BF16),
            pltpu.VMEM((hops, far, 2, rows, half), BF16),
            pltpu.VMEM((rows, half), F32),
            pltpu.VMEM((2, rows, half), F32),
            pltpu.VMEM((mid, rows, half), BF16),
            pltpu.VMEM((2, rows, half), F32),
            pltpu.VMEM((mid, 2, 8, rows), F32),
            pltpu.VMEM((mid, 2, 8, rows), F32),
            pltpu.VMEM((mid, n_dst, 2, 8, rows), F32),
            pltpu.VMEM((mid, 2, rows, half), BF16),
            pltpu.VMEM((mid, rows, half), BF16),
            dma((5,)),
            dma((2 + 2 * hops,)),
            dma((n_dst,)),
            dma((n_dst,)),
            dma((hops, n_dst, 2)),
            dma((hops, n_dst, 2)),
            dma((hops, far, 2)),
            dma((hops, far, 2)),
            dma((mid, n_dst)),
            dma((mid, n_dst)),
            dma((3 * hops + 2,)),
            dma((3 * hops + 2,)),
        ],
        compiler_params=pltpu.CompilerParams(
            collective_id=0, has_side_effects=True, vmem_limit_bytes=60 * 1024 * 1024
        ),
    )(raw, enc_w1, enc_w2, block_weights, block_cols, noise)
    shapes = (
        jax.ShapeDtypeStruct((rows, width), BF16),
        jax.ShapeDtypeStruct((hops, rows, width), BF16),
    )
    return pl.pallas_call(
        finish,
        out_shape=shapes,
        in_specs=[anywhere, anywhere],
        out_specs=(anywhere, anywhere),
        scratch_shapes=[pltpu.VMEM(s.shape, BF16) for s in shapes] + [dma((4,))],
    )(encoded, kept)


def solution(mesh):
    placed = (
        P(("src", "dst"), None),
        P(),
        P(),
        P(("src", "dst"), None, None),
        P(("src", "dst")),
        P(None, ("src", "dst"), None),
    )
    return jax.shard_map(
        functools.partial(shards, mesh.shape["src"], mesh.shape["dst"]),
        mesh=mesh,
        in_specs=placed,
        out_specs=(P(("src", "dst"), None), P(None, ("src", "dst"), None)),
        check_vma=False,
    )
```

time: 47.1 us -> 45.5 us (0.966)
  Pallas kernels: 46.3 us -> 44.7 us
    pallas_call x1, Pallas kernels: 44.6 us -> 43.1 us  [shards(): pl.pallas_call(functools.partial(kernel, n_src, n_dst, hops), out_shape=(...]
where the time goes in v1:
time: 45.5 us; the launch traced here: 45.4 us
  Pallas kernels  44.7 us (98%)
  between operations  0.64 us (1%)
    pallas_call x1, Pallas kernels, shards(): pl.pallas_call(functools.partial(kernel, n_src, n_dst, hops), out_shape=(...  43.1 us
    pallas_call x1, Pallas kernels, shards(): pl.pallas_call(finish, out_shape=shapes, in_specs=[anywhere, anywhere], o...  1.66 us

profile of v1, /device:TPU:0, one launch (start us, length us, event | category | flops | bytes accessed | tf_op | source)
XLA Modules:
  0.0 45.4 jit_solution(3057754105997726547)
XLA Ops:
  0.6 43.1 %shard_map.77 = (bf16[128,256]{1,0:T(8,128)(2,1)}, bf16[3,128,256]{2,1,0:T(8,128)(2,1)}) custom-call(bf16[128,256]{1,0:T(8,128)(2,1)} %raw_h.1, bf16[256,512]{1,0:T(8,128)(2,1)} %w1_h.1, bf16[512,256]{1,0:T(8,128)(2,1)} %w2_h.1, f32[16,128,128]{2,1,0:T(8,128)} %bw_h.1, s32[16]{0:T(128)} %cols.1, bf16[3,128,256]{2,1,0:T(8,128)(2,1)} %noise_h.1), custom_call_target="tpu_custom_call" | custom-call | tf_op jit(solution)/shard_map/pallas_call | solution.py:342
  43.7 1.7 %shard_map.78 = (bf16[128,256]{1,0:T(8,128)(2,1)}, bf16[3,128,256]{2,1,0:T(8,128)(2,1)}) custom-call(bf16[128,256]{1,0:T(8,128)(2,1)} %get-tuple-element.4.enc_i, bf16[3,128,256]{2,1,0:T(8,128)(2,1)} %get-tuple-element.5.hops_i), custom_call_target="tpu_custom_call" | custom-call | tf_op jit(solution)/shard_map/pallas_call | solution.py:395

commit v2 on v1

--- a/solution.py
+++ b/solution.py
@@ -20,12 +20,12 @@
 
 def kernel(
     n_src, n_dst, hops,
-    raw_h, w1_h, w2_h, bw_h, cols, noise_h,
-    enc_h, hops_h,
-    raw_v, w1_v, w2_v, bw_v, noise_v, enc_v, last_v,
+    raw_h, w1_h, w2_h, bw_h, cols_h, noise_h,
+    enc_v, hops_v,
+    raw_v, w1_v, w2_v, bw_v, noise_v, cols,
     dense, scaled, gath, cross, acc, out, inn, near_out, near_in,
-    noise_p, zs, stat_out, stat_in, scale, kept, kept_in,
-    load_sem, store_sem, w_send, w_recv, g_send, g_recv, r_send, r_recv, s_send, s_recv, p_send, p_recv,
+    noise_p, zs, ends, stat_out, stat_in, scale, kept, kept_in,
+    load_sem, w_send, w_recv, g_send, g_recv, r_send, r_recv, s_send, s_recv, p_send, p_recv,
 ):
     src, dst = lax.axis_index("src"), lax.axis_index("dst")
     pairs = n_src // 2
@@ -51,7 +51,14 @@
     loads = [
         pltpu.make_async_copy(a, b, load_sem.at[i])
         for i, (a, b) in enumerate(
-            ((raw_h, raw_v), (w1_h, w1_v), (w2_h, w2_v), (bw_h, bw_v), (noise_h, noise_v))
+            (
+                (raw_h, raw_v),
+                (w1_h, w1_v),
+                (w2_h, w2_v),
+                (bw_h, bw_v),
+                (noise_h, noise_v),
+                (cols_h, cols),
+            )
         )
     ]
     for load in loads:
@@ -82,6 +89,8 @@
         sent.append(copy)
         return copy
 
+    middle = [n_dst // 2] if n_dst > 1 else []
+    rest = [step for step in range(1, n_dst) if step not in middle]
     far_first = list(reversed(range(1, n_dst)))
 
     loads[0].wait()
@@ -95,7 +104,7 @@
     cross[...] = jnp.where(core == 0, feats[:, half:], feats[:, :half])
     pl.semaphore_wait(barrier, greeted)
     first = {}
-    for step, rel in [(step, rel) for step in far_first for rel in (0, 1)] + [(0, 1)]:
+    for step, rel in [(step, rel) for step in middle + rest[::-1] for rel in (1, 0)] + [(0, 1)]:
         first[step, rel] = start(
             remote(
                 cross if rel else gath.at[0, dst, core],
@@ -106,10 +115,9 @@
             )
         )
     enc_v[...] = feats
-    stores = [pltpu.make_async_copy(enc_v, enc_h, store_sem.at[0])]
-    stores[0].start()
 
     loads[3].wait()
+    loads[5].wait()
     weights = []
     blocks = [[bw_v[r * per_row + i].astype(BF16) for i in range(per_row)] for r in range(n_src)]
     for step in range(n_dst):
@@ -153,6 +161,7 @@
     data = {}
     scales = {}
     pending = None
+    kept_copies = []
     scatter_steps = list(reversed(range(1, pairs))) + [0]
     for hop in range(hops):
         for step in range(n_dst):
@@ -206,16 +215,16 @@
                         )
                     )
                     continue
-                rel = 1 - u
+                rel = u
                 r = at_core(to, rel)
                 y = product(r) + acc[r]
                 if step == 0 and rel == 0:
-                    zs[core] = y
+                    ends[core] = y
                 elif step == 0:
                     near_out[...] = y
                     copies[0, 1] = start(
                         remote(
-                            near_out, zs.at[core], p_send.at[3 * hops + 1], p_recv.at[3 * hops + 1], {"src": partner}
+                            near_out, ends.at[core], p_send.at[3 * hops + 1], p_recv.at[3 * hops + 1], {"src": partner}
                         )
                     )
                 else:
@@ -230,17 +239,15 @@
                         )
                     )
         if hop == last:
-            for copy in copies.values():
-                copy.wait_recv()
-            sums = []
-            for h in range(2):
-                z = zs[h] + noise_v[hop, :, h * half : (h + 1) * half].astype(F32)
-                for step in range(1, pairs):
-                    z = z + inn[hop, step - 1, h].astype(F32)
-                sums.append(z)
-            last_v[...] = normalized(jnp.concatenate(sums, axis=1))
-            stores.append(pltpu.make_async_copy(last_v, hops_h.at[hop], store_sem.at[1]))
-            stores[-1].start()
+            copies[0, 1].wait_recv()
+            sums = [ends[h] + noise_v[hop, :, h * half : (h + 1) * half].astype(F32) for h in range(2)]
+            for rel in (0, 1):
+                for step in scatter_steps[:-1]:
+                    copies[step, rel].wait_recv()
+                    if rel:
+                        for h in range(2):
+                            sums[h] = sums[h] + inn[hop, step - 1, h].astype(F32)
+            hops_v[hop] = normalized(jnp.concatenate(sums, axis=1))
             continue
         if hop == 0:
             noise_copy.wait_recv()
@@ -252,7 +259,7 @@
                 copies[step, u].wait_recv()
                 z = z + inn[hop, step - 1, u].astype(F32)
             gath[hop + 1, dst, u] = z.astype(BF16)
-            for step in far_first:
+            for step in middle + rest:
                 data[hop + 1, step, u] = start(
                     remote(
                         gath.at[hop + 1, dst, u],
@@ -284,46 +291,32 @@
             for u in (0, 1):
                 column = jnp.transpose(jnp.broadcast_to(scale[hop, dst, u, 0:1], (rows, rows)))
                 kept[hop, u] = (zs[u] * column).astype(BF16)
-            copy = start(
-                remote(
-                    kept.at[hop, 1 - core],
-                    kept_in.at[hop],
-                    p_send.at[hops + hop],
-                    p_recv.at[hops + hop],
-                    {"src": partner},
+            hops_v[hop, :, lanes(core)] = kept[hop, core]
+            kept_copies.append(
+                start(
+                    remote(
+                        kept.at[hop, 1 - core],
+                        kept_in.at[hop],
+                        p_send.at[hops + hop],
+                        p_recv.at[hops + hop],
+                        {"src": partner},
+                    )
                 )
             )
-            store = pltpu.make_async_copy(
-                kept.at[hop, core], hops_h.at[hop, :, lanes(core)], store_sem.at[2 + 2 * hop]
-            )
-            store.start()
-            stores.append(store)
-            copy.wait_recv()
-            store = pltpu.make_async_copy(
-                kept_in.at[hop], hops_h.at[hop, :, lanes(1 - core)], store_sem.at[3 + 2 * hop]
-            )
-            store.start()
-            stores.append(store)
-
+
+    for hop, copy in enumerate(kept_copies):
+        copy.wait_recv()
+        hops_v[hop, :, lanes(1 - core)] = kept_in[hop]
     for copy in sent:
         copy.wait_send()
-    for store in stores:
-        store.wait()
-
-
-def finish(enc_i, hops_i, enc_o, hops_o, enc_v, hops_v, sem):
-    reads = [
-        pltpu.make_async_copy(hops_i, hops_v, sem.at[0]),
-        pltpu.make_async_copy(enc_i, enc_v, sem.at[1]),
+
+
+def finish(enc_i, hops_i, enc_o, hops_o, sem):
+    writes = [
+        pltpu.make_async_copy(hops_i, hops_o, sem.at[0]),
+        pltpu.make_async_copy(enc_i, enc_o, sem.at[1]),
     ]
-    writes = [
-        pltpu.make_async_copy(hops_v, hops_o, sem.at[2]),
-        pltpu.make_async_copy(enc_v, enc_o, sem.at[3]),
-    ]
-    for read in reads:
-        read.start()
-    for read, write in zip(reads, writes):
-        read.wait()
+    for write in writes:
         write.start()
     for write in writes:
         write.wait()
@@ -336,25 +329,22 @@
     half = width // 2
     assert rows == side and n_src % 2 == 0
     anywhere = pl.BlockSpec(memory_space=pl.ANY)
+    inside = pl.BlockSpec(memory_space=pltpu.VMEM)
     dma = pltpu.SemaphoreType.DMA
     far = max(pairs - 1, 1)
     mid = max(hops - 1, 1)
     encoded, kept = pl.pallas_call(
         functools.partial(kernel, n_src, n_dst, hops),
-        out_shape=(
-            jax.ShapeDtypeStruct((rows, width), BF16),
-            jax.ShapeDtypeStruct((hops, rows, width), BF16),
-        ),
-        in_specs=[anywhere] * 4 + [pl.BlockSpec(memory_space=pltpu.SMEM), anywhere],
-        out_specs=(anywhere, anywhere),
+        out_shape=(pltpu.VMEM((rows, width), BF16), pltpu.VMEM((hops, rows, width), BF16)),
+        in_specs=[anywhere] * 6,
+        out_specs=(inside, inside),
         scratch_shapes=[
             pltpu.VMEM(raw.shape, BF16),
             pltpu.VMEM(enc_w1.shape, BF16),
             pltpu.VMEM(enc_w2.shape, BF16),
             pltpu.VMEM(block_weights.shape, F32),
             pltpu.VMEM(noise.shape, BF16),
-            pltpu.VMEM((rows, width), BF16),
-            pltpu.VMEM((rows, width), BF16),
+            pltpu.SMEM(block_cols.shape, jnp.int32),
             pltpu.VMEM((n_dst, 2, n_src, side, side), BF16),
             pltpu.VMEM((n_src, side, 2 * side), BF16),
             pltpu.VMEM((hops, n_dst, 2, rows, half), BF16),
@@ -366,13 +356,13 @@
             pltpu.VMEM((2, rows, half), F32),
             pltpu.VMEM((mid, rows, half), BF16),
             pltpu.VMEM((2, rows, half), F32),
+            pltpu.VMEM((2, rows, half), F32),
             pltpu.VMEM((mid, 2, 8, rows), F32),
             pltpu.VMEM((mid, 2, 8, rows), F32),
             pltpu.VMEM((mid, n_dst, 2, 8, rows), F32),
             pltpu.VMEM((mid, 2, rows, half), BF16),
             pltpu.VMEM((mid, rows, half), BF16),
-            dma((5,)),
-            dma((2 + 2 * hops,)),
+            dma((6,)),
             dma((n_dst,)),
             dma((n_dst,)),
             dma((hops, n_dst, 2)),
@@ -395,10 +385,10 @@
     return pl.pallas_call(
         finish,
         out_shape=shapes,
-        in_specs=[anywhere, anywhere],
+        in_specs=[inside, inside],
         out_specs=(anywhere, anywhere),
-        scratch_shapes=[pltpu.VMEM(s.shape, BF16) for s in shapes] + [dma((4,))],
-    )(encoded, kept)
+        scratch_shapes=[dma((2,))],
+    )(*(pltpu.with_memory_space_constraint(a, pltpu.VMEM) for a in (encoded, kept)))
 
 
 def solution(mesh):

time: 45.5 us -> 40.2 us (0.88)
  Pallas kernels: 44.7 us -> 39.4 us
    pallas_call x1, Pallas kernels: 43.1 us -> 38.7 us  [shards(): pl.pallas_call(functools.partial(kernel, n_src, n_dst, hops), out_shape=(...]
    pallas_call x1, Pallas kernels: 1.66 us -> 0.71 us  [shards(): pl.pallas_call(finish, out_shape=shapes, in_specs=[inside, inside], out_s...]
where the time goes in v2:
time: 40.2 us; the launch traced here: 40.1 us
  Pallas kernels  39.4 us (98%)
  between operations  0.64 us (2%)
    pallas_call x1, Pallas kernels, shards(): pl.pallas_call(functools.partial(kernel, n_src, n_dst, hops), out_shape=(...  38.7 us

profile of v2, /device:TPU:0, one launch (start us, length us, event | category | flops | bytes accessed | tf_op | source)
XLA Modules:
  0.0 40.1 jit_solution(4625472144866025463)
XLA Ops:
  0.6 38.7 %shard_map.77 = (bf16[128,256]{1,0:T(8,128)(2,1)S(1)}, bf16[3,128,256]{2,1,0:T(8,128)(2,1)S(1)}) custom-call(bf16[128,256]{1,0:T(8,128)(2,1)} %raw_h.1, bf16[256,512]{1,0:T(8,128)(2,1)} %w1_h.1, bf16[512,256]{1,0:T(8,128)(2,1)} %w2_h.1, f32[16,128,128]{2,1,0:T(8,128)} %bw_h.1, s32[16]{0:T(128)} %cols_h.1, bf16[3,128,256]{2,1,0:T(8,128)(2,1)} %noise_h.1), custom_call_target="tpu_custom_call" | custom-call | tf_op jit(solution)/shard_map/pallas_call | solution.py:336
  39.4 0.7 %shard_map.78 = (bf16[128,256]{1,0:T(8,128)(2,1)}, bf16[3,128,256]{2,1,0:T(8,128)(2,1)}) custom-call(bf16[128,256]{1,0:T(8,128)(2,1)S(1)} %get-tuple-element.4.enc_i, bf16[3,128,256]{2,1,0:T(8,128)(2,1)S(1)} %get-tuple-element.5.hops_i), custom_call_target="tpu_custom_call" | custom-call | tf_op jit(solution)/shard_map/pallas_call | solution.py:385

commit v3 on v2

--- a/solution.py
+++ b/solution.py
@@ -171,7 +171,7 @@
             else:
                 if step:
                     scales[hop, step].wait_recv()
-                by = jnp.concatenate([scale[hop - 1, c, 0, 0:1], scale[hop - 1, c, 1, 0:1]], axis=1)
+                by = jnp.concatenate([scale[hop - 1, c, u : u + 1] for u in (0, 1)], axis=1)
                 for r in range(n_src):
                     w = jnp.concatenate([dense[c, 0, r], dense[c, 1, r]], axis=1)
                     scaled[r] = (w.astype(F32) * by).astype(BF16)
@@ -252,6 +252,7 @@
         if hop == 0:
             noise_copy.wait_recv()
         z_values = []
+        totals = []
         for u in (0, 1):
             own_noise = noise_v[hop, :, lanes(core)]
             z = near_in[u] + jnp.where(core == u, own_noise, noise_p[hop]).astype(F32)
@@ -270,7 +271,9 @@
                     )
                 )
             zs[u] = z
-            stat_out[hop, u] = row_sums(z)
+            totals.append(row_sums(z))
+        first_row = lax.broadcasted_iota(jnp.int32, totals[0].shape, 0) == 0
+        stat_out[hop] = jnp.where(first_row, totals[0], totals[1])
         stats = start(
             remote(stat_out.at[hop], stat_in.at[hop], p_send.at[hop], p_recv.at[hop], {"src": partner})
         )
@@ -289,7 +292,7 @@
 
         def pending(hop=hop):
             for u in (0, 1):
-                column = jnp.transpose(jnp.broadcast_to(scale[hop, dst, u, 0:1], (rows, rows)))
+                column = jnp.transpose(jnp.broadcast_to(scale[hop, dst, u : u + 1], (rows, rows)))
                 kept[hop, u] = (zs[u] * column).astype(BF16)
             hops_v[hop, :, lanes(core)] = kept[hop, core]
             kept_copies.append(
@@ -357,9 +360,9 @@
             pltpu.VMEM((mid, rows, half), BF16),
             pltpu.VMEM((2, rows, half), F32),
             pltpu.VMEM((2, rows, half), F32),
-            pltpu.VMEM((mid, 2, 8, rows), F32),
-            pltpu.VMEM((mid, 2, 8, rows), F32),
-            pltpu.VMEM((mid, n_dst, 2, 8, rows), F32),
+            pltpu.VMEM((mid, 8, rows), F32),
+            pltpu.VMEM((mid, 8, rows), F32),
+            pltpu.VMEM((mid, n_dst, 8, rows), F32),
             pltpu.VMEM((mid, 2, rows, half), BF16),
             pltpu.VMEM((mid, rows, half), BF16),
             dma((6,)),

time: 40.2 us -> 39.7 us (0.988)
  Pallas kernels: 39.4 us -> 38.9 us
    pallas_call x1, Pallas kernels: 38.7 us -> 38.2 us  [shards(): pl.pallas_call(functools.partial(kernel, n_src, n_dst, hops), out_shape=(...]
where the time goes in v3:
time: 39.7 us; the launch traced here: 39.6 us
  Pallas kernels  38.9 us (98%)
  between operations  0.64 us (2%)
    pallas_call x1, Pallas kernels, shards(): pl.pallas_call(functools.partial(kernel, n_src, n_dst, hops), out_shape=(...  38.2 us

profile of v3, /device:TPU:0, one launch (start us, length us, event | category | flops | bytes accessed | tf_op | source)
XLA Modules:
  0.0 39.6 jit_solution(826334454021695433)
XLA Ops:
  0.6 38.2 %shard_map.77 = (bf16[128,256]{1,0:T(8,128)(2,1)S(1)}, bf16[3,128,256]{2,1,0:T(8,128)(2,1)S(1)}) custom-call(bf16[128,256]{1,0:T(8,128)(2,1)} %raw_h.1, bf16[256,512]{1,0:T(8,128)(2,1)} %w1_h.1, bf16[512,256]{1,0:T(8,128)(2,1)} %w2_h.1, f32[16,128,128]{2,1,0:T(8,128)} %bw_h.1, s32[16]{0:T(128)} %cols_h.1, bf16[3,128,256]{2,1,0:T(8,128)(2,1)} %noise_h.1), custom_call_target="tpu_custom_call" | custom-call | tf_op jit(solution)/shard_map/pallas_call | solution.py:339
  38.8 0.7 %shard_map.78 = (bf16[128,256]{1,0:T(8,128)(2,1)}, bf16[3,128,256]{2,1,0:T(8,128)(2,1)}) custom-call(bf16[128,256]{1,0:T(8,128)(2,1)S(1)} %get-tuple-element.4.enc_i, bf16[3,128,256]{2,1,0:T(8,128)(2,1)S(1)} %get-tuple-element.5.hops_i), custom_call_target="tpu_custom_call" | custom-call | tf_op jit(solution)/shard_map/pallas_call | solution.py:388
